TPU v7x, 32 devices: a whole 2x2x4 slice. The times are simulated.
32 devices in a mesh: dp: 8 (over y, x, core), tensor: 4 (over z).
Axes of the slice: x: 2, y: 2, z: 4, core: 2. Of those that a mesh axis runs over, the one named last changes fastest.
Arguments:
- block_input: float32 [8, 736, 1152], P('dp', 'tensor'), may hold values from -6 to 6
- key_valid: int32 [8, 736], P('dp'), may hold values from 0 to 1, as said below
- mixgain: bfloat16 [2, 1152], P(None, 'dp'), may hold values from 0.5 to 1.5
- mixbias: bfloat16 [2, 1152], P(None, 'dp'), may hold values from -3 to 3
- inproj_weight: bfloat16 [2, 3, 1152, 1152], P(None, None, 'dp', 'tensor'), may hold values from -1 to 1
- querybias: bfloat16 [2, 1152], P(None, 'tensor'), may hold values from -3 to 3
- valuebias: bfloat16 [2, 1152], P(None, 'tensor'), may hold values from -3 to 3
- outproj_weight: bfloat16 [2, 1152, 1152], P(None, 'tensor', 'dp'), may hold values from -3 to 3
- outbias: bfloat16 [2, 1152], P(None, 'dp'), may hold values from -3 to 3
- ffgain: bfloat16 [2, 1152], P(None, 'dp'), may hold values from 0.5 to 1.5
- ffbias: bfloat16 [2, 1152], P(None, 'dp'), may hold values from -3 to 3
- expand_weight: bfloat16 [2, 1152, 4304], P(None, 'dp', 'tensor'), may hold values from -0.1875 to 0.1875
- expbias: bfloat16 [2, 4304], P(None, 'tensor'), may hold values from -3 to 3
- contract_weight: bfloat16 [2, 4304, 1152], P(None, 'tensor', 'dp'), may hold values from -0.25 to 0.25
- conbias: bfloat16 [2, 1152], P(None, 'dp'), may hold values from -4 to 4
- cotangent: float32 [8, 736, 1152], P('dp', 'tensor'), may hold values from -6 to 6
Outputs:
- block_output: float32 [8, 736, 1152], P('dp', 'tensor')
- input_gradient: float32 [8, 736, 1152], P('dp', 'tensor')
- mixgain_gradient: float32 [2, 1152], P(None, 'dp')
- mixbias_gradient: float32 [2, 1152], P(None, 'dp')
- inproj_gradient: float32 [2, 3, 1152, 1152], P(None, None, 'dp', 'tensor')
- querybias_gradient: float32 [2, 1152], P(None, 'tensor')
- valuebias_gradient: float32 [2, 1152], P(None, 'tensor')
- outproj_gradient: float32 [2, 1152, 1152], P(None, 'tensor', 'dp')
- outbias_gradient: float32 [2, 1152], P(None, 'dp')
- ffgain_gradient: float32 [2, 1152], P(None, 'dp')
- ffbias_gradient: float32 [2, 1152], P(None, 'dp')
- expand_gradient: float32 [2, 1152, 4304], P(None, 'dp', 'tensor')
- expbias_gradient: float32 [2, 4304], P(None, 'tensor')
- contract_gradient: float32 [2, 4304, 1152], P(None, 'tensor', 'dp')
- conbias_gradient: float32 [2, 1152], P(None, 'dp')
Inputs may be any that keep to these rules, and one draw needn't show every extreme that they name: `key_valid`: each image's row is 1 on a first run of positions and 0 after it; every image has from 552 to 736 ones, and both ends occur in every draw.
All inputs are finite; a program needn't handle non-finite values.
Results may differ from a plain program's by a relative error of at most 0.033.
Values may be sent and summed in bfloat16 or wider, within the bound.
A program may use at most 192 MiB of HBM per device.

v0:
```python
import jax
import jax.numpy as jnp
from jax import lax
from jax.sharding import PartitionSpec as P

HEAD_DIM = 72
norm_epsilon = 1e-06
gelu_scale = 0.7978845608028654
gelu_cubic = 0.044715
masked_score = -1e30


def layer_norm(matrix_rows, norm_gain, norm_shift):
    centered = matrix_rows - jnp.mean(matrix_rows, axis=-1, keepdims=True)
    inverse = lax.rsqrt(jnp.mean(centered * centered, axis=-1, keepdims=True) + norm_epsilon)
    normed = centered * inverse
    return (
        normed * norm_gain.astype(jnp.float32) + norm_shift.astype(jnp.float32),
        normed,
        inverse,
    )


def norm_backward(upstream, normed, inverse, norm_gain):
    scaled = upstream * norm_gain.astype(jnp.float32)
    mean_first = jnp.mean(scaled, axis=-1, keepdims=True)
    mean_second = jnp.mean(scaled * normed, axis=-1, keepdims=True)
    return inverse * (scaled - mean_first - normed * mean_second)


def gelu_parts(preact):
    tanh_part = jnp.tanh(gelu_scale * (preact + gelu_cubic * preact * preact * preact))
    gelu_value = 0.5 * preact * (1.0 + tanh_part)
    gelu_slope = 0.5 * (1.0 + tanh_part) + 0.5 * preact * (
        1.0 - tanh_part * tanh_part
    ) * gelu_scale * (1.0 + 3.0 * gelu_cubic * preact * preact)
    return (gelu_value, gelu_slope)


def masked_scores(queries, keys_half, usable, factor):
    scores = (
        jnp.einsum("bqhd,bkhd->bhqk", queries, keys_half, preferred_element_type=jnp.float32)
        * factor
    )
    return jnp.where(usable[:, None, None, :], scores, masked_score)


def attend(queries, keys_half, values_half, usable, factor):
    scores = masked_scores(queries, keys_half, usable, factor)
    highest = jnp.max(scores, axis=-1, keepdims=True)
    log_total = highest + jnp.log(jnp.sum(jnp.exp(scores - highest), axis=-1, keepdims=True))
    weights = jnp.exp(scores - log_total).astype(jnp.bfloat16)
    mixed_out = jnp.einsum(
        "bhqk,bkhd->bqhd", weights, values_half, preferred_element_type=jnp.float32
    )
    return (mixed_out.astype(jnp.bfloat16), log_total)


def attend_backward(queries, keys_half, values_half, usable, log_total, upstream, factor):
    weights = jnp.exp(masked_scores(queries, keys_half, usable, factor) - log_total)
    value_grad = jnp.einsum(
        "bhqk,bqhd->bkhd",
        weights.astype(jnp.bfloat16),
        upstream,
        preferred_element_type=jnp.float32,
    )
    weight_grad = jnp.einsum(
        "bqhd,bkhd->bhqk", upstream, values_half, preferred_element_type=jnp.float32
    )
    inner_sum = jnp.sum(weights * weight_grad, axis=-1, keepdims=True)
    score_grad = (weights * (weight_grad - inner_sum) * factor).astype(jnp.bfloat16)
    query_grad = jnp.einsum(
        "bhqk,bkhd->bqhd", score_grad, keys_half, preferred_element_type=jnp.float32
    )
    key_grad = jnp.einsum(
        "bhqk,bqhd->bkhd", score_grad, queries, preferred_element_type=jnp.float32
    )
    return (query_grad, key_grad, value_grad)


def body(
    block_input,
    key_valid,
    mixgain,
    mixbias,
    inproj_weight,
    querybias,
    valuebias,
    outproj_weight,
    outbias,
    ffgain,
    ffbias,
    expand_weight,
    expbias,
    contract_weight,
    conbias,
    cotangent,
):
    images = block_input.shape[0]
    model_width = block_input.shape[2]
    seq_total = key_valid.shape[1]
    depth_count = inproj_weight.shape[0]
    local_width = inproj_weight.shape[-1]
    local_heads = local_width // HEAD_DIM
    local_hidden = expand_weight.shape[-1]
    hidden_total = local_hidden * lax.axis_size("tensor")
    shard_width = model_width // lax.axis_size("dp")
    factor = float(HEAD_DIM) ** (-0.5)
    usable = key_valid > 0
    tensor_index = lax.axis_index("tensor")
    data_index = lax.axis_index("dp")
    head_shape = (images, seq_total, local_heads, HEAD_DIM)

    def fetch_attention(layer_index):
        return (
            lax.all_gather(inproj_weight[layer_index], "dp", axis=1, tiled=True),
            lax.all_gather(outproj_weight[layer_index], "dp", axis=1, tiled=True),
            lax.all_gather(mixgain[layer_index], "dp", axis=0, tiled=True),
            lax.all_gather(mixbias[layer_index], "dp", axis=0, tiled=True),
            lax.all_gather(outbias[layer_index], "dp", axis=0, tiled=True),
        )

    def fetch_dense(layer_index):
        return (
            lax.all_gather(expand_weight[layer_index], "dp", axis=0, tiled=True),
            lax.all_gather(contract_weight[layer_index], "dp", axis=1, tiled=True),
            lax.all_gather(ffgain[layer_index], "dp", axis=0, tiled=True),
            lax.all_gather(ffbias[layer_index], "dp", axis=0, tiled=True),
            lax.all_gather(conbias[layer_index], "dp", axis=0, tiled=True),
        )

    residual = block_input
    stored = []
    for layer_index in range(depth_count):
        attention_pack = fetch_attention(layer_index)
        inproj_full, outproj_full, mix_gain, mix_shift, out_shift = attention_pack
        mix_value, mix_normed, mix_inverse = layer_norm(residual, mix_gain, mix_shift)
        mix_rows = lax.all_gather(mix_value.astype(jnp.bfloat16), "tensor", axis=1, tiled=True)
        projected = jnp.einsum(
            "bsd,cde->cbse", mix_rows, inproj_full, preferred_element_type=jnp.float32
        )
        queries = (
            (projected[0] + querybias[layer_index].astype(jnp.float32))
            .astype(jnp.bfloat16)
            .reshape(head_shape)
        )
        keys_half = projected[1].astype(jnp.bfloat16).reshape(head_shape)
        values_half = (
            (projected[2] + valuebias[layer_index].astype(jnp.float32))
            .astype(jnp.bfloat16)
            .reshape(head_shape)
        )
        heads_out, log_total = attend(queries, keys_half, values_half, usable, factor)
        heads_flat = heads_out.reshape(images, seq_total, local_width)
        partial_out = jnp.einsum(
            "bse,ed->bsd", heads_flat, outproj_full, preferred_element_type=jnp.float32
        )
        middle = (
            residual
            + lax.psum_scatter(
                partial_out.astype(jnp.bfloat16), "tensor", scatter_dimension=1, tiled=True
            ).astype(jnp.float32)
            + out_shift.astype(jnp.float32)
        )
        dense_pack = fetch_dense(layer_index)
        expand_full, contract_full, ff_gain, ff_shift, con_shift = dense_pack
        ff_value, ff_normed, ff_inverse = layer_norm(middle, ff_gain, ff_shift)
        ff_rows = lax.all_gather(ff_value.astype(jnp.bfloat16), "tensor", axis=1, tiled=True)
        preact = jnp.einsum(
            "bsd,df->bsf", ff_rows, expand_full, preferred_element_type=jnp.float32
        ) + expbias[layer_index].astype(jnp.float32)
        gelu_value, gelu_slope = gelu_parts(preact)
        hidden_half = gelu_value.astype(jnp.bfloat16)
        partial_dense = jnp.einsum(
            "bsf,fd->bsd", hidden_half, contract_full, preferred_element_type=jnp.float32
        )
        stored.append(
            (
                mix_normed,
                mix_inverse,
                mix_rows,
                queries,
                keys_half,
                values_half,
                log_total,
                heads_flat,
                ff_normed,
                ff_inverse,
                ff_rows,
                gelu_slope,
                hidden_half,
                attention_pack,
                dense_pack,
            )
        )
        residual = (
            middle
            + lax.psum_scatter(
                partial_dense.astype(jnp.bfloat16), "tensor", scatter_dimension=1, tiled=True
            ).astype(jnp.float32)
            + con_shift.astype(jnp.float32)
        )
    upstream = cotangent
    layer_results = [None] * depth_count
    for layer_index in reversed(range(depth_count)):
        (
            mix_normed,
            mix_inverse,
            mix_rows,
            queries,
            keys_half,
            values_half,
            log_total,
            heads_flat,
            ff_normed,
            ff_inverse,
            ff_rows,
            gelu_slope,
            hidden_half,
            attention_pack,
            dense_pack,
        ) = stored[layer_index]
        expand_full, contract_full, ff_gain, ff_shift, con_shift = fetch_dense(layer_index)
        upstream_half = upstream.astype(jnp.bfloat16)
        upstream_rows = lax.all_gather(upstream_half, "tensor", axis=1, tiled=True)
        contract_grad = jnp.einsum(
            "bsf,bsd->fd", hidden_half, upstream_rows, preferred_element_type=jnp.float32
        )
        preact_grad = (
            jnp.einsum(
                "bsd,fd->bsf", upstream_rows, contract_full, preferred_element_type=jnp.float32
            )
            * gelu_slope
        )
        preact_half = preact_grad.astype(jnp.bfloat16)
        expand_grad = jnp.einsum(
            "bsd,bsf->df", ff_rows, preact_half, preferred_element_type=jnp.float32
        )
        ff_partial = jnp.einsum(
            "bsf,df->bsd", preact_half, expand_full, preferred_element_type=jnp.float32
        )
        ff_back = lax.psum_scatter(
            ff_partial.astype(jnp.bfloat16), "tensor", scatter_dimension=1, tiled=True
        ).astype(jnp.float32)
        middle_grad = upstream + norm_backward(ff_back, ff_normed, ff_inverse, ff_gain)
        inproj_full, outproj_full, mix_gain, mix_shift, out_shift = fetch_attention(layer_index)
        middle_rows = lax.all_gather(middle_grad.astype(jnp.bfloat16), "tensor", axis=1, tiled=True)
        outproj_grad = jnp.einsum(
            "bse,bsd->ed", heads_flat, middle_rows, preferred_element_type=jnp.float32
        )
        heads_grad = (
            jnp.einsum("bsd,ed->bse", middle_rows, outproj_full, preferred_element_type=jnp.float32)
            .astype(jnp.bfloat16)
            .reshape(head_shape)
        )
        query_grad, key_grad, value_grad = attend_backward(
            queries, keys_half, values_half, usable, log_total, heads_grad, factor
        )
        proj_grad = jnp.stack([query_grad, key_grad, value_grad]).reshape(
            3, images, seq_total, local_width
        )
        proj_half = proj_grad.astype(jnp.bfloat16)
        inproj_grad = jnp.einsum(
            "bsd,cbse->cde", mix_rows, proj_half, preferred_element_type=jnp.float32
        )
        mix_partial = jnp.einsum(
            "cbse,cde->bsd", proj_half, inproj_full, preferred_element_type=jnp.float32
        )
        mix_back = lax.psum_scatter(
            mix_partial.astype(jnp.bfloat16), "tensor", scatter_dimension=1, tiled=True
        ).astype(jnp.float32)
        upstream_next = middle_grad + norm_backward(mix_back, mix_normed, mix_inverse, mix_gain)
        query_full = lax.dynamic_update_slice(
            jnp.zeros((model_width,), jnp.float32),
            jnp.sum(proj_grad[0], axis=(0, 1)),
            (tensor_index * local_width,),
        )
        value_full = lax.dynamic_update_slice(
            jnp.zeros((model_width,), jnp.float32),
            jnp.sum(proj_grad[2], axis=(0, 1)),
            (tensor_index * local_width,),
        )
        expand_full_bias = lax.dynamic_update_slice(
            jnp.zeros((hidden_total,), jnp.float32),
            jnp.sum(preact_grad, axis=(0, 1)),
            (tensor_index * local_hidden,),
        )
        vector_rows = jnp.stack(
            [
                jnp.sum(mix_back * mix_normed, axis=(0, 1)),
                jnp.sum(mix_back, axis=(0, 1)),
                jnp.sum(middle_grad, axis=(0, 1)),
                jnp.sum(ff_back * ff_normed, axis=(0, 1)),
                jnp.sum(ff_back, axis=(0, 1)),
                jnp.sum(upstream, axis=(0, 1)),
                query_full,
                value_full,
            ]
        )
        local_grads = (inproj_grad, outproj_grad, expand_grad, contract_grad)
        weight_parts = (
            lax.psum_scatter(
                local_grads[0].astype(jnp.bfloat16), "dp", scatter_dimension=1, tiled=True
            ).astype(jnp.float32),
            lax.psum_scatter(
                local_grads[1].astype(jnp.bfloat16), "dp", scatter_dimension=1, tiled=True
            ).astype(jnp.float32),
            lax.psum_scatter(
                local_grads[2].astype(jnp.bfloat16), "dp", scatter_dimension=0, tiled=True
            ).astype(jnp.float32),
            lax.psum_scatter(
                local_grads[3].astype(jnp.bfloat16), "dp", scatter_dimension=1, tiled=True
            ).astype(jnp.float32),
        )
        layer_results[layer_index] = (weight_parts, vector_rows, expand_full_bias)
        upstream = upstream_next
    inproj_list = []
    outproj_list = []
    expand_list = []
    contract_list = []
    vector_list = []
    expbias_list = []
    for position in range(depth_count):
        weight_parts, vector_rows, expand_full_bias = layer_results[position]
        inproj_list.append(weight_parts[0])
        outproj_list.append(weight_parts[1])
        expand_list.append(weight_parts[2])
        contract_list.append(weight_parts[3])
        vector_list.append(vector_rows)
        expbias_list.append(expand_full_bias)
    inproj_out, outproj_out, expand_out, contract_out = (
        jnp.stack(inproj_list),
        jnp.stack(outproj_list),
        jnp.stack(expand_list),
        jnp.stack(contract_list),
    )
    vector_total, expbias_total = lax.psum(
        (jnp.stack(vector_list), jnp.stack(expbias_list)), ("dp", "tensor")
    )
    data_part = lax.dynamic_slice_in_dim(vector_total, data_index * shard_width, shard_width, 2)
    tensor_part = lax.dynamic_slice_in_dim(vector_total, tensor_index * local_width, local_width, 2)
    expbias_part = lax.dynamic_slice_in_dim(
        expbias_total, tensor_index * local_hidden, local_hidden, 1
    )
    return (
        residual,
        upstream,
        data_part[:, 0],
        data_part[:, 1],
        inproj_out,
        tensor_part[:, 6],
        tensor_part[:, 7],
        outproj_out,
        data_part[:, 2],
        data_part[:, 3],
        data_part[:, 4],
        expand_out,
        expbias_part,
        contract_out,
        data_part[:, 5],
    )


def solution(mesh):
    return jax.shard_map(
        body,
        mesh=mesh,
        in_specs=(
            P("dp", "tensor", None),
            P("dp", None),
            P(None, "dp"),
            P(None, "dp"),
            P(None, None, "dp", "tensor"),
            P(None, "tensor"),
            P(None, "tensor"),
            P(None, "tensor", "dp"),
            P(None, "dp"),
            P(None, "dp"),
            P(None, "dp"),
            P(None, "dp", "tensor"),
            P(None, "tensor"),
            P(None, "tensor", "dp"),
            P(None, "dp"),
            P("dp", "tensor", None),
        ),
        out_specs=(
            P("dp", "tensor", None),
            P("dp", "tensor", None),
            P(None, "dp"),
            P(None, "dp"),
            P(None, None, "dp", "tensor"),
            P(None, "tensor"),
            P(None, "tensor"),
            P(None, "tensor", "dp"),
            P(None, "dp"),
            P(None, "dp"),
            P(None, "dp"),
            P(None, "dp", "tensor"),
            P(None, "tensor"),
            P(None, "tensor", "dp"),
            P(None, "dp"),
        ),
        check_vma=False,
    )
```

profile of v0, /device:TPU:8, one launch (start us, length us, event | category | flops | bytes accessed | tf_op | source)
XLA Modules:
  0.0 1475.8 jit_solution(15815517332685027929)
XLA Ops:
  19.3 24.6 %all-reduce.20 = (bf16[1152]{0:T(1024)(128)(2,1)S(1)}, bf16[1152]{0:T(1024)(128)(2,1)S(1)}, bf16[1152]{0:T(1024)(128)(2,1)S(1)}, bf16[1152]{0:T(1024)(128)(2,1)S...) all-reduce(bf16[1152]{0:T(1024)(128)(2,1)S(1)} %dynamic-update-slic, ...), channel_id=3, replica_groups=mesh['dp'=8,'tensor'=4] {'dp'}, use_global_device_ids=true, to_apply=%add.1 | all-reduce | flops 13824 | bytes 55296
  48.1 9.9 all-gather.3
  58.0 26.2 %all-gather.35.cloned.1.call-done = bf16[1,736,1152]{2,1,0:T(8,128)(2,1)} async-done(((bf16[1,184,1152]{2,1,0:T(8,128)(2,1)}), bf16[1,736,1152]{2,1,0:T(8,128)(2,1)}) %all-gather.35.cloned.1.call-update) | async-done | bytes 1695760 | tf_op jit(solution)/shard_map/all_gather | solution.py:138
  84.2 32.5 %all-gather.51.cloned.1.call-done = bf16[1,3,1152,288]{3,2,1,0:T(8,128)(2,1)} async-done(((bf16[1,3,144,288]{3,2,1,0:T(8,128)(2,1)}), bf16[1,3,1152,288]{3,2,1,0:T(8,128)(2,1)}) %all-gather.51.cloned.1.call-update) | async-done | bytes 1990672 | tf_op jit(solution)/shard_map/all_gather | solution.py:116
  116.7 4.2 fusion.92
  135.5 35.5 %reduce-scatter.61.cloned.1.call-done = bf16[1,184,1152]{2,1,0:T(8,128)(2,1)} async-done(((bf16[1,736,1152]{2,1,0:T(8,128)(2,1)}), bf16[1,184,1152]{2,1,0:T(8,128)(2,1)}) %reduce-scatter.61.cloned.1.call-update) | async-done | bytes 423952
  175.1 28.4 %all-gather.53.cloned.1.call-done = bf16[1,1152,1076]{2,1,0:T(8,128)(2,1)} async-done(((bf16[1,144,1076]{2,1,0:T(8,128)(2,1)}), bf16[1,1152,1076]{2,1,0:T(8,128)(2,1)}) %all-gather.53.cloned.1.call-update) | async-done | bytes 2479120 | tf_op jit(solution)/shard_map/all_gather | solution.py:125
  203.5 40.1 %all-gather.37.cloned.1.call-done = bf16[1,736,1152]{2,1,0:T(8,128)(2,1)} async-done(((bf16[1,184,1152]{2,1,0:T(8,128)(2,1)}), bf16[1,736,1152]{2,1,0:T(8,128)(2,1)}) %all-gather.37.cloned.1.call-update) | async-done | bytes 1695760 | tf_op jit(solution)/shard_map/all_gather | solution.py:168
  243.5 6.3 convolution_add_fusion.1
  249.8 25.4 %all-gather.55.cloned.1.call-done = bf16[1,1076,1152]{1,2,0:T(8,128)(2,1)} async-done(((bf16[1,1076,144]{1,2,0:T(8,128)(2,1)}), bf16[1,1076,1152]{1,2,0:T(8,128)(2,1)}) %all-gather.55.cloned.1.call-update) | async-done | bytes 2479120 | tf_op jit(solution)/shard_map/all_gather | solution.py:126
  275.3 7.2 fusion.70
  283.3 35.7 %reduce-scatter.63.cloned.1.call-done = bf16[1,184,1152]{2,1,0:T(8,128)(2,1)} async-done(((bf16[1,736,1152]{2,1,0:T(8,128)(2,1)}), bf16[1,184,1152]{2,1,0:T(8,128)(2,1)}) %reduce-scatter.63.cloned.1.call-update) | async-done | bytes 423952
  321.7 12.8 all-gather.13
  334.5 17.2 %all-gather.57.cloned.1.call-done = bf16[1,3,1152,288]{3,2,1,0:T(8,128)(2,1)} async-done(((bf16[1,3,144,288]{3,2,1,0:T(8,128)(2,1)}), bf16[1,3,1152,288]{3,2,1,0:T(8,128)(2,1)}) %all-gather.57.cloned.1.call-update) | async-done | bytes 1990672 | tf_op jit(solution)/shard_map/all_gather | solution.py:116
  351.6 40.2 %all-gather.39.cloned.1.call-done = bf16[1,736,1152]{2,1,0:T(8,128)(2,1)} async-done(((bf16[1,184,1152]{2,1,0:T(8,128)(2,1)}), bf16[1,736,1152]{2,1,0:T(8,128)(2,1)}) %all-gather.39.cloned.1.call-update) | async-done | bytes 1695760 | tf_op jit(solution)/shard_map/all_gather | solution.py:138
  391.9 4.3 fusion.95
  409.7 35.6 %reduce-scatter.65.cloned.1.call-done = bf16[1,184,1152]{2,1,0:T(8,128)(2,1)} async-done(((bf16[1,736,1152]{2,1,0:T(8,128)(2,1)}), bf16[1,184,1152]{2,1,0:T(8,128)(2,1)}) %reduce-scatter.65.cloned.1.call-update) | async-done | bytes 423952
  451.0 26.9 %all-gather.59.cloned.1.call-done = bf16[1,1152,1076]{2,1,0:T(8,128)(2,1)} async-done(((bf16[1,144,1076]{2,1,0:T(8,128)(2,1)}), bf16[1,1152,1076]{2,1,0:T(8,128)(2,1)}) %all-gather.59.cloned.1.call-update) | async-done | bytes 2479120 | tf_op jit(solution)/shard_map/all_gather | solution.py:125
  477.9 40.1 %all-gather.41.cloned.1.call-done = bf16[1,736,1152]{2,1,0:T(8,128)(2,1)} async-done(((bf16[1,184,1152]{2,1,0:T(8,128)(2,1)}), bf16[1,736,1152]{2,1,0:T(8,128)(2,1)}) %all-gather.41.cloned.1.call-update) | async-done | bytes 1695760 | tf_op jit(solution)/shard_map/all_gather | solution.py:168
  518.0 6.4 convolution_add_fusion
  524.4 33.7 %all-gather.43.cloned.1.call-done = bf16[1,736,1152]{2,1,0:T(8,128)(2,1)} async-done(((bf16[1,184,1152]{2,1,0:T(8,128)(2,1)}), bf16[1,736,1152]{2,1,0:T(8,128)(2,1)}) %all-gather.43.cloned.1.call-update) | async-done | bytes 1695760 | tf_op jit(solution)/shard_map/all_gather | solution.py:225
  558.0 31.7 %all-gather.61.cloned.1.call-done = bf16[1,1076,1152]{1,2,0:T(8,128)(2,1)} async-done(((bf16[1,1076,144]{1,2,0:T(8,128)(2,1)}), bf16[1,1076,1152]{1,2,0:T(8,128)(2,1)}) %all-gather.61.cloned.1.call-update) | async-done | bytes 2479120 | tf_op jit(solution)/shard_map/all_gather | solution.py:126
  589.8 8.2 fusion.232
  599.2 4.0 fusion.72
  603.7 7.2 fusion.71
  610.9 28.8 %reduce-scatter.69.cloned.1.call-done = bf16[1,184,1152]{2,1,0:T(8,128)(2,1)} async-done(((bf16[1,736,1152]{2,1,0:T(8,128)(2,1)}), bf16[1,184,1152]{2,1,0:T(8,128)(2,1)}) %reduce-scatter.69.cloned.1.call-update) | async-done | bytes 423952
  641.8 36.5 %reduce-scatter.67.cloned.1.call-done = bf16[1,184,1152]{2,1,0:T(8,128)(2,1)} async-done(((bf16[1,736,1152]{2,1,0:T(8,128)(2,1)}), bf16[1,184,1152]{2,1,0:T(8,128)(2,1)}) %reduce-scatter.67.cloned.1.call-update) | async-done | bytes 423952
  678.4 3.3 fusion.212
  683.4 38.2 %all-gather.45.cloned.1.call-done = bf16[1,736,1152]{2,1,0:T(8,128)(2,1)} async-done(((bf16[1,184,1152]{2,1,0:T(8,128)(2,1)}), bf16[1,736,1152]{2,1,0:T(8,128)(2,1)}) %all-gather.45.cloned.1.call-update) | async-done | bytes 1695760 | tf_op jit(solution)/shard_map/all_gather | solution.py:247
  724.1 5.1 fusion.221
  729.1 5.0 fusion.176
  734.1 17.1 %fusion.122 = bf16[4,72,736]{2,1,0:T(8,128)(2,1)S(1)} fusion(f32[4,736,736]{1,2,0:T(8,128)} %fusion.176, f32[4,736,736]{1,2,0:T(8,128)} %copy-done.1, f32[4,736]{1,0:T(4,128)S(1)} %log_add_fusion, pred[736]{0:T(1024)(128)(4,1)S(1)} %compare_reduce_fusion, f32[736,4,72]{0,2,1:T(8,128)} %bitcast.272, f32[4,72]{1,0:T(4,128)S(1)} %reshape.789), kind=kOutput, calls=%fused_computation.138 | convolution fusion | flops 336491104 | bytes 18619744 | tf_op jit(solution)/shard_map/bhqk,bqhd->bkhd/dot_general | solution.py:75
  751.3 18.1 %fusion.222 = (f32[4,72]{1,0:T(4,128)}, bf16[1,736,4,72]{1,3,2,0:T(8,128)(2,1)}) fusion(bf16[736,4,72]{0,2,1:T(8,128)(2,1)S(1)} %bitcast.282, f32[4,736,736]{1,2,0:T(8,128)} %fusion.176, f32[4,736,736]{1,2,0:T(8,128)} %copy-done.1, f32[4,736]{1,0:T(4,128)S(1)} %log_add_fusion, pred[736]{0:T(1024)(128)(4,1)S(1)} %compare_reduce_fusion), kind=kOutput, calls=%fused_computation.295 | convolution fusion | flops 336278848 | bytes 18195808 | tf_op jit(solution)/shard_map/bhqk,bkhd->bqhd/dot_general | solution.py:72
  769.4 5.8 fusion.75
  775.3 36.3 %reduce-scatter.71.cloned.1.call-done = bf16[1,184,1152]{2,1,0:T(8,128)(2,1)} async-done(((bf16[1,736,1152]{2,1,0:T(8,128)(2,1)}), bf16[1,184,1152]{2,1,0:T(8,128)(2,1)}) %reduce-scatter.71.cloned.1.call-update) | async-done | bytes 423952
  816.8 38.0 %all-gather.47.cloned.1.call-done = bf16[1,736,1152]{2,1,0:T(8,128)(2,1)} async-done(((bf16[1,184,1152]{2,1,0:T(8,128)(2,1)}), bf16[1,736,1152]{2,1,0:T(8,128)(2,1)}) %all-gather.47.cloned.1.call-update) | async-done | bytes 1695760 | tf_op jit(solution)/shard_map/all_gather | solution.py:225
  854.8 8.2 fusion.233
  864.2 4.0 fusion.73
  868.3 36.3 %reduce-scatter.73.cloned.1.call-done = bf16[1,184,1152]{2,1,0:T(8,128)(2,1)} async-done(((bf16[1,736,1152]{2,1,0:T(8,128)(2,1)}), bf16[1,184,1152]{2,1,0:T(8,128)(2,1)}) %reduce-scatter.73.cloned.1.call-update) | async-done | bytes 423952
  910.4 4.8 fusion.69
  915.3 6.0 copy.81
  921.3 4.2 reshape.929
  926.0 6.7 convolution_convert_fusion
  932.8 6.2 convolution_convert_fusion.1
  939.0 6.2 convolution_convert_fusion.2
  945.4 5.6 convolution_convert_fusion.3
  951.0 3.6 convolution_convert_fusion.12
  957.2 5.1 fusion.174
  962.3 16.6 %fusion.125 = bf16[4,72,736]{2,1,0:T(8,128)(2,1)S(1)} fusion(f32[4,736,736]{1,2,0:T(8,128)} %fusion.174, f32[4,736,736]{1,2,0:T(8,128)} %copy-done, f32[4,736]{1,0:T(4,128)S(1)} %copy-done.36, pred[736]{0:T(1024)(128)(4,1)S(1)} %compare_reduce_fusion, f32[736,4,72]{0,2,1:T(8,128)S(1)} %bitcast.270, f32[4,72]{1,0:T(4,128)S(1)} %copy-done.55), kind=kOutput, calls=%fused_computation.139 | convolution fusion | flops 336491104 | bytes 18619744 | tf_op jit(solution)/shard_map/bhqk,bqhd->bkhd/dot_general | solution.py:75
  979.0 3.7 convolution_convert_fusion.13
  982.7 17.4 %fusion.220 = (f32[4,72]{1,0:T(4,128)}, bf16[1,736,4,72]{1,3,2,0:T(8,128)(2,1)S(1)}) fusion(bf16[736,4,72]{0,2,1:T(8,128)(2,1)S(1)} %bitcast.280, f32[4,736,736]{1,2,0:T(8,128)} %fusion.174, f32[4,736,736]{1,2,0:T(8,128)} %copy-done, f32[4,736]{1,0:T(4,128)S(1)} %copy-done.36, pred[736]{0:T(1024)(128)(4,1)S(1)} %compare_reduce_fusion), kind=kOutput, calls=%fused_computation.293 | convolution fusion | flops 336278848 | bytes 18195808 | tf_op jit(solution)/shard_map/bhqk,bkhd->bqhd/dot_general | solution.py:72
  1000.1 4.8 fusion.219
  1008.9 6.0 copy.79
  1014.9 4.2 reshape.927
  1019.5 6.1 fusion.74
  1030.5 40.0 %psum.15 = f32[2,4304]{1,0:T(2,128)S(1)} all-reduce(f32[2,4304]{1,0:T(2,128)S(1)} %pad_maximum_fusion.7), channel_id=1, replica_groups=mesh['dp'=8,'tensor'=4] {'dp','tensor'}, use_global_device_ids=true, to_apply=%region_55.56 | all-reduce | flops 8608 | bytes 68864 | tf_op jit(solution)/shard_map/psum | solution.py:337
  1071.2 14.6 reduce-scatter.53.cloned.1.call-done
  1088.0 44.3 %reduce-scatter.51.cloned.1.call-done = bf16[144,1076]{1,0:T(8,128)(2,1)} async-done(((bf16[1152,1076]{1,0:T(8,128)(2,1)}), bf16[144,1076]{1,0:T(8,128)(2,1)}) %reduce-scatter.51.cloned.1.call-update) | async-done | bytes 309904 | tf_op jit(solution)/shard_map/reduce_scatter | solution.py:308
  1132.3 46.4 %reduce-scatter.49.cloned.1.call-done = bf16[144,1076]{1,0:T(8,128)(2,1)} async-done(((bf16[1152,1076]{1,0:T(8,128)(2,1)}), bf16[144,1076]{1,0:T(8,128)(2,1)}) %reduce-scatter.49.cloned.1.call-update) | async-done | bytes 309904 | tf_op jit(solution)/shard_map/reduce_scatter | solution.py:308
  1183.4 33.1 %reduce-scatter.47.cloned.1.call-done = bf16[288,144]{0,1:T(8,128)(2,1)} async-done(((bf16[288,1152]{0,1:T(8,128)(2,1)}), bf16[288,144]{0,1:T(8,128)(2,1)}) %reduce-scatter.47.cloned.1.call-update) | async-done | bytes 82960 | tf_op jit(solution)/shard_map/reduce_scatter | solution.py:305
  1216.4 38.5 %reduce-scatter.45.cloned.1.call-done = bf16[288,144]{0,1:T(8,128)(2,1)} async-done(((bf16[288,1152]{0,1:T(8,128)(2,1)}), bf16[288,144]{0,1:T(8,128)(2,1)}) %reduce-scatter.45.cloned.1.call-update) | async-done | bytes 82960 | tf_op jit(solution)/shard_map/reduce_scatter | solution.py:305
  1256.7 41.8 %reduce-scatter.57.cloned.1.call-done = bf16[144,864]{1,0:T(8,128)(2,1)} async-done(((bf16[1152,864]{1,0:T(8,128)(2,1)}), bf16[144,864]{1,0:T(8,128)(2,1)}) %reduce-scatter.57.cloned.1.call-update) | async-done | bytes 248848
  1304.3 32.7 %reduce-scatter.75.cloned.1.call-done = bf16[1,184,1152]{2,1,0:T(8,128)(2,1)} async-done(((bf16[1,736,1152]{2,1,0:T(8,128)(2,1)}), bf16[1,184,1152]{2,1,0:T(8,128)(2,1)}) %reduce-scatter.75.cloned.1.call-update) | async-done | bytes 423952
  1342.3 123.6 %all-reduce.23.cloned.1.call-done = f32[2,8,1152]{2,0,1:T(2,128)} async-done(((f32[2,8,1152]{2,0,1:T(2,128)}), f32[2,8,1152]{2,0,1:T(2,128)}) %all-reduce.23.cloned.1.call-update) | async-done | bytes 73744 | tf_op jit(solution)/shard_map/psum | solution.py:337
  (373 shorter events, 112.2 us)
Async XLA Ops:
  7.2 39.6 %copy-start.26 = (bf16[2,3,144,288]{3,2,1,0:T(8,128)(2,1)S(1)}, bf16[2,3,144,288]{3,2,1,0:T(8,128)(2,1)}, u32[]{:S(2)}) copy-start(bf16[2,3,144,288]{3,2,1,0:T(8,128)(2,1)} %param.20) | copy-start | bytes 1492996
  7.2 40.6 %copy-start.58 = (bf16[2,288]{1,0:T(2,128)(2,1)S(1)}, bf16[2,288]{1,0:T(2,128)(2,1)}, u32[]{:S(2)}) copy-start(bf16[2,288]{1,0:T(2,128)(2,1)} %param.21) | copy-start | bytes 3460
  7.2 40.7 %copy-start.59 = (bf16[2,288]{1,0:T(2,128)(2,1)S(1)}, bf16[2,288]{1,0:T(2,128)(2,1)}, u32[]{:S(2)}) copy-start(bf16[2,288]{1,0:T(2,128)(2,1)} %param.22) | copy-start | bytes 3460
  7.2 40.8 %copy-start.60 = (s32[1,736]{1,0:T(1,128)S(1)}, s32[1,736]{1,0:T(1,128)}, u32[]{:S(2)}) copy-start(s32[1,736]{1,0:T(1,128)} %param.17) | copy-start | bytes 8836
  7.2 40.8 %copy-start.32 = (bf16[2,288,144]{1,2,0:T(8,128)(2,1)S(1)}, bf16[2,288,144]{1,2,0:T(8,128)(2,1)}, u32[]{:S(2)}) copy-start(bf16[2,288,144]{1,2,0:T(8,128)(2,1)} %param.23) | copy-start | bytes 497668
  7.2 77.0 %all-gather.35.cloned.1.call-start = ((), (), s32[]{:S(2)}) async-start(), calls=%async_computation.16 | async-start | bytes 2119680 | tf_op jit(solution)/shard_map/all_gather | solution.py:138
  8.6 39.5 %copy-start.46 = (f32[184]{0:T(256)}, f32[184]{0:T(256)S(1)}, u32[]{:S(2)}) copy-start(f32[184]{0:T(256)S(1)} %broadcast_multiply_fusion.11) | copy-start | bytes 2212
  10.1 38.0 %copy-start.50 = (f32[184]{0:T(256)}, f32[184]{0:T(256)S(1)}, u32[]{:S(2)}) copy-start(f32[184]{0:T(256)S(1)} %add_rsqrt_fusion.3) | copy-start | bytes 2212
  46.7 69.9 %all-gather.51.cloned.1.call-start = ((), (), s32[]{:S(2)}) async-start(), calls=%async_computation.31 | async-start | bytes 2985984 | tf_op jit(solution)/shard_map/all_gather | solution.py:116
  47.7 123.2 %reduce-scatter.61.cloned.1.call-start = ((), (), s32[]{:S(2)}) async-start(), calls=%async_computation.39 | async-start | bytes 2119680
  47.9 73.2 %copy-start.54 = (f32[4,72]{1,0:T(4,128)}, f32[4,72]{1,0:T(4,128)S(1)}, u32[]{:S(2)}) copy-start(f32[4,72]{1,0:T(4,128)S(1)} %reshape.786) | copy-start | bytes 3460
  58.0 73.3 %copy-start.23 = (bf16[1,288,1152]{1,2,0:T(8,128)(2,1)}, bf16[1,288,1152]{1,2,0:T(8,128)(2,1)S(1)}, u32[]{:S(2)}) copy-start(bf16[1,288,1152]{1,2,0:T(8,128)(2,1)S(1)} %all-gather.3) | copy-start | bytes 1990660
  131.3 39.7 %copy-start.4 = (f32[1,184,1152]{2,1,0:T(8,128)S(1)}, f32[1,184,1152]{2,1,0:T(8,128)}, u32[]{:S(2)}) copy-start(f32[1,184,1152]{2,1,0:T(8,128)} %param.16) | copy-start | bytes 2543620
  134.4 39.0 %copy-start.28 = (bf16[2,1076,144]{1,2,0:T(8,128)(2,1)S(1)}, bf16[2,1076,144]{1,2,0:T(8,128)(2,1)}, u32[]{:S(2)}) copy-start(bf16[2,1076,144]{1,2,0:T(8,128)(2,1)} %param.29) | copy-start | bytes 1859332
  134.4 69.0 %all-gather.53.cloned.1.call-start = ((), (), s32[]{:S(2)}) async-start(), calls=%async_computation.32 | async-start | bytes 2985984 | tf_op jit(solution)/shard_map/all_gather | solution.py:125
  135.4 39.6 %copy-start.49 = (bf16[2,1076]{1,0:T(2,128)(2,1)S(1)}, bf16[2,1076]{1,0:T(2,128)(2,1)}, u32[]{:S(2)}) copy-start(bf16[2,1076]{1,0:T(2,128)(2,1)} %param.28) | copy-start | bytes 12916
  135.4 108.1 %all-gather.37.cloned.1.call-start = ((), (), s32[]{:S(2)}) async-start(), calls=%async_computation.17 | async-start | bytes 2119680 | tf_op jit(solution)/shard_map/all_gather | solution.py:168
  173.4 101.8 %all-gather.55.cloned.1.call-start = ((), (), s32[]{:S(2)}) async-start(), calls=%async_computation.33 | async-start | bytes 2985984 | tf_op jit(solution)/shard_map/all_gather | solution.py:126
  174.5 144.5 %reduce-scatter.63.cloned.1.call-start = ((), (), s32[]{:S(2)}) async-start(), calls=%async_computation.40 | async-start | bytes 2119680
  282.5 69.2 %all-gather.57.cloned.1.call-start = ((), (), s32[]{:S(2)}) async-start(), calls=%async_computation.34 | async-start | bytes 2985984 | tf_op jit(solution)/shard_map/all_gather | solution.py:116
  283.2 108.7 %all-gather.39.cloned.1.call-start = ((), (), s32[]{:S(2)}) async-start(), calls=%async_computation.18 | async-start | bytes 2119680 | tf_op jit(solution)/shard_map/all_gather | solution.py:138
  321.5 123.8 %reduce-scatter.65.cloned.1.call-start = ((), (), s32[]{:S(2)}) async-start(), calls=%async_computation.41 | async-start | bytes 2119680
  408.9 69.0 %all-gather.59.cloned.1.call-start = ((), (), s32[]{:S(2)}) async-start(), calls=%async_computation.35 | async-start | bytes 2985984 | tf_op jit(solution)/shard_map/all_gather | solution.py:125
  409.6 108.3 %all-gather.41.cloned.1.call-start = ((), (), s32[]{:S(2)}) async-start(), calls=%async_computation.19 | async-start | bytes 2119680 | tf_op jit(solution)/shard_map/all_gather | solution.py:168
  447.7 110.3 %all-gather.43.cloned.1.call-start = ((), (), s32[]{:S(2)}) async-start(), calls=%async_computation.20 | async-start | bytes 2119680 | tf_op jit(solution)/shard_map/all_gather | solution.py:225
  450.1 139.6 %all-gather.61.cloned.1.call-start = ((), (), s32[]{:S(2)}) async-start(), calls=%async_computation.36 | async-start | bytes 2985984 | tf_op jit(solution)/shard_map/all_gather | solution.py:126
  450.7 189.0 %reduce-scatter.69.cloned.1.call-start = ((), (), s32[]{:S(2)}) async-start(), calls=%async_computation.43 | async-start | bytes 2119680
  589.8 9.4 copy-start.64
  603.2 75.2 %reduce-scatter.67.cloned.1.call-start = ((), (), s32[]{:S(2)}) async-start(), calls=%async_computation.42 | async-start | bytes 2119680
  610.8 110.7 %all-gather.45.cloned.1.call-start = ((), (), s32[]{:S(2)}) async-start(), calls=%async_computation.21 | async-start | bytes 2119680 | tf_op jit(solution)/shard_map/all_gather | solution.py:247
  683.4 128.3 %reduce-scatter.71.cloned.1.call-start = ((), (), s32[]{:S(2)}) async-start(), calls=%async_computation.44 | async-start | bytes 2119680
  734.1 17.1 %copy-start.18 = (bf16[1,1,736,288]{2,3,0,1:T(8,128)(2,1)S(1)}, bf16[1,1,736,288]{2,3,0,1:T(8,128)(2,1)}, u32[]{:S(2)}) copy-start(bf16[1,1,736,288]{2,3,0,1:T(8,128)(2,1)} %copy-done.17) | copy-start | bytes 1271812
  751.2 18.2 %copy-start.68 = (bf16[4,72,736]{2,1,0:T(8,128)(2,1)}, bf16[4,72,736]{2,1,0:T(8,128)(2,1)S(1)}, u32[]{:S(2)}) copy-start(bf16[4,72,736]{2,1,0:T(8,128)(2,1)S(1)} %fusion.122) | copy-start | bytes 1271812
  751.2 18.2 %copy-start.29 = (bf16[1,736,4,72]{1,3,2,0:T(8,128)(2,1)S(1)}, bf16[1,736,4,72]{1,3,2,0:T(8,128)(2,1)}, u32[]{:S(2)}) copy-start(bf16[1,736,4,72]{1,3,2,0:T(8,128)(2,1)} %get-tuple-element.112) | copy-start | bytes 1271812
  775.2 38.5 %copy-start.11 = (f32[1,184,1152]{2,1,0:T(8,128)S(1)}, f32[1,184,1152]{2,1,0:T(8,128)}, u32[]{:S(2)}) copy-start(f32[1,184,1152]{2,1,0:T(8,128)} %copy-done.10) | copy-start | bytes 2543620
  775.3 79.5 %all-gather.47.cloned.1.call-start = ((), (), s32[]{:S(2)}) async-start(), calls=%async_computation.22 | async-start | bytes 2119680 | tf_op jit(solution)/shard_map/all_gather | solution.py:225
  816.5 88.0 %reduce-scatter.73.cloned.1.call-start = ((), (), s32[]{:S(2)}) async-start(), calls=%async_computation.45 | async-start | bytes 2119680
  854.7 9.4 copy-start.63
  868.2 42.2 %copy-start.30 = (bf16[1,736,4,72]{1,3,2,0:T(8,128)(2,1)S(1)}, bf16[1,736,4,72]{1,3,2,0:T(8,128)(2,1)}, u32[]{:S(2)}) copy-start(bf16[1,736,4,72]{1,3,2,0:T(8,128)(2,1)} %get-tuple-element.112) | copy-start | bytes 1271812
  868.2 42.2 %copy-start.69 = (bf16[4,72,736]{2,1,0:T(8,128)(2,1)S(1)}, bf16[4,72,736]{2,1,0:T(8,128)(2,1)}, u32[]{:S(2)}) copy-start(bf16[4,72,736]{2,1,0:T(8,128)(2,1)} %copy-done.68) | copy-start | bytes 1271812
  868.2 86.7 %all-gather.49.cloned.1.call-start = ((), (), s32[]{:S(2)}) async-start(), calls=%async_computation.23 | async-start | bytes 2119680 | tf_op jit(solution)/shard_map/all_gather | solution.py:247
  910.4 116.7 %reduce-scatter.59.cloned.1.call-start = ((), (), s32[]{:S(2)}) async-start(), calls=%async_computation.38 | async-start | bytes 2322432
  925.6 145.7 %reduce-scatter.55.cloned.1.call-start = ((), (), s32[]{:S(2)}) async-start(), calls=%async_computation.30 | async-start | bytes 2985984 | tf_op jit(solution)/shard_map/reduce_scatter | solution.py:311
  932.7 153.1 %reduce-scatter.53.cloned.1.call-start = ((), (), s32[]{:S(2)}) async-start(), calls=%async_computation.29 | async-start | bytes 2985984 | tf_op jit(solution)/shard_map/reduce_scatter | solution.py:311
  939.0 193.3 %reduce-scatter.51.cloned.1.call-start = ((), (), s32[]{:S(2)}) async-start(), calls=%async_computation.28 | async-start | bytes 2985984 | tf_op jit(solution)/shard_map/reduce_scatter | solution.py:308
  945.3 233.4 %reduce-scatter.49.cloned.1.call-start = ((), (), s32[]{:S(2)}) async-start(), calls=%async_computation.27 | async-start | bytes 2985984 | tf_op jit(solution)/shard_map/reduce_scatter | solution.py:308
  951.0 265.5 %reduce-scatter.47.cloned.1.call-start = ((), (), s32[]{:S(2)}) async-start(), calls=%async_computation.26 | async-start | bytes 995328 | tf_op jit(solution)/shard_map/reduce_scatter | solution.py:305
  954.7 300.2 %reduce-scatter.45.cloned.1.call-start = ((), (), s32[]{:S(2)}) async-start(), calls=%async_computation.25 | async-start | bytes 995328 | tf_op jit(solution)/shard_map/reduce_scatter | solution.py:305
  962.3 16.6 %copy-start.20 = (bf16[4,72,736]{2,1,0:T(8,128)(2,1)S(1)}, bf16[4,72,736]{2,1,0:T(8,128)(2,1)}, u32[]{:S(2)}) copy-start(bf16[4,72,736]{2,1,0:T(8,128)(2,1)} %copy-done.19) | copy-start | bytes 1271812
  978.9 26.0 %copy-start.70 = (bf16[4,72,736]{2,1,0:T(8,128)(2,1)}, bf16[4,72,736]{2,1,0:T(8,128)(2,1)S(1)}, u32[]{:S(2)}) copy-start(bf16[4,72,736]{2,1,0:T(8,128)(2,1)S(1)} %fusion.125) | copy-start | bytes 1271812
  982.7 315.8 %reduce-scatter.57.cloned.1.call-start = ((), (), s32[]{:S(2)}) async-start(), calls=%async_computation.37 | async-start | bytes 2322432
  1019.2 317.8 %reduce-scatter.75.cloned.1.call-start = ((), (), s32[]{:S(2)}) async-start(), calls=%async_computation.46 | async-start | bytes 2119680
  1025.5 45.6 %copy-start.44 = (f32[1152]{0:T(1024)S(1)}, f32[1152]{0:T(1024)}, u32[]{:S(2)}) copy-start(f32[1152]{0:T(1024)} %get-tuple-element.45) | copy-start | bytes 13828
  1025.6 45.6 %copy-start.45 = (f32[1152]{0:T(1024)S(1)}, f32[1152]{0:T(1024)}, u32[]{:S(2)}) copy-start(f32[1152]{0:T(1024)} %get-tuple-element.93) | copy-start | bytes 13828
  1025.6 45.6 %copy-start.43 = (f32[1152]{0:T(1024)S(1)}, f32[1152]{0:T(1024)}, u32[]{:S(2)}) copy-start(f32[1152]{0:T(1024)} %get-tuple-element.57) | copy-start | bytes 13828
  1025.6 155.3 %copy-start.53 = (f32[4,72]{1,0:T(4,128)S(1)}, f32[4,72]{1,0:T(4,128)}, u32[]{:S(2)}) copy-start(f32[4,72]{1,0:T(4,128)} %get-tuple-element.107) | copy-start | bytes 3460
  1025.6 155.4 %copy-start.62 = (f32[4,72]{1,0:T(4,128)S(1)}, f32[4,72]{1,0:T(4,128)}, u32[]{:S(2)}) copy-start(f32[4,72]{1,0:T(4,128)} %get-tuple-element.109) | copy-start | bytes 3460
  1025.6 440.3 %all-reduce.23.cloned.1.call-start = ((), (), s32[]{:S(2)}) async-start(), calls=%async_computation.24 | async-start | bytes 147456 | tf_op jit(solution)/shard_map/psum | solution.py:337
  1183.4 116.7 %copy-start.48 = (f32[1,1152]{1,0:T(1,128)}, f32[1,1152]{1,0:T(1,128)S(1)}, u32[]{:S(2)}) copy-start(f32[1,1152]{1,0:T(1,128)S(1)} %dynamic_update_slice.24) | copy-start | bytes 13828
  1300.0 37.0 %copy-start.5 = (f32[1,184,1152]{2,1,0:T(8,128)S(1)}, f32[1,184,1152]{2,1,0:T(8,128)}, u32[]{:S(2)}) copy-start(f32[1,184,1152]{2,1,0:T(8,128)} %param.16) | copy-start | bytes 2543620
  1300.0 37.0 %copy-start.34 = (f32[1152]{0:T(1024)S(1)}, f32[1152]{0:T(1024)}, u32[]{:S(2)}) copy-start(f32[1152]{0:T(1024)} %copy-done.33) | copy-start | bytes 13828
  1300.0 37.0 %copy-start.47 = (f32[184]{0:T(256)S(1)}, f32[184]{0:T(256)}, u32[]{:S(2)}) copy-start(f32[184]{0:T(256)} %copy-done.46) | copy-start | bytes 2212
  1300.1 37.0 %copy-start.51 = (f32[184]{0:T(256)S(1)}, f32[184]{0:T(256)}, u32[]{:S(2)}) copy-start(f32[184]{0:T(256)} %copy-done.50) | copy-start | bytes 2212
  1301.2 38.9 %copy-start.9 = (f32[1,184,1152]{2,1,0:T(8,128)S(1)}, f32[1,184,1152]{2,1,0:T(8,128)}, u32[]{:S(2)}) copy-start(f32[1,184,1152]{2,1,0:T(8,128)} %copy-done.8) | copy-start | bytes 2543620
  (41 other events, 164.1 us)
Sparse Core Ops, SparseCore 0:
  46.9 37.3 all-gather.34
  86.7 29.9 all-gather.50
  134.6 36.3 reduce-scatter.60
  173.3 30.1 all-gather.52
  205.5 38.0 all-gather.36
  245.3 29.9 all-gather.54
  282.6 36.3 reduce-scatter.62
  321.5 30.1 all-gather.56
  353.8 38.0 all-gather.38
  409.0 36.2 reduce-scatter.64
  447.7 30.1 all-gather.58
  479.9 38.0 all-gather.40
  520.1 37.8 all-gather.42
  559.8 29.9 all-gather.60
  603.3 36.3 reduce-scatter.68
  641.9 36.4 reduce-scatter.66
  683.5 38.0 all-gather.44
  775.4 36.2 reduce-scatter.70
  816.7 38.0 all-gather.46
  868.3 36.2 reduce-scatter.72
  910.5 38.0 all-gather.48
  951.9 39.9 reduce-scatter.58
  995.4 43.1 reduce-scatter.54
  1042.0 43.7 reduce-scatter.52
  1089.3 42.9 reduce-scatter.50
  1135.7 42.9 reduce-scatter.48
  1181.8 34.6 reduce-scatter.46
  1220.3 34.6 reduce-scatter.44
  1258.3 40.0 reduce-scatter.56
  1300.6 36.3 reduce-scatter.74
  1342.6 123.3 all-reduce.22
where the time goes:
time: 1480 us
  waiting for transfers between devices  1040 us (70%)
  matrix products  217 us (15%)
  blocking collectives  87.3 us (6%)
  local copies, waits for them, and re-layouts  59.3 us (4%)
  other arithmetic  51.7 us (3%)
  between operations  16.7 us (1%)
    unnamed x41, waiting for transfers between devices  321 us
    psum x1, waiting for transfers between devices, body(): lax.psum((jnp.stack(vector_list), jnp.stack(expbias_list)), ('dp', 'tenso...  124 us
    reduce_scatter x2, waiting for transfers between devices, body(): lax.psum_scatter(local_grads[2].astype(jnp.bfloat16), 'dp', scatter_dimen...  90.6 us
    all_gather x2, waiting for transfers between devices, body(): lax.all_gather(ff_value.astype(jnp.bfloat16), 'tensor', axis=1, tiled=True)  80.1 us
    all_gather x2, waiting for transfers between devices, body(): upstream_rows = lax.all_gather(upstream_half, 'tensor', axis=1, tiled=True)  71.6 us
    reduce_scatter x2, waiting for transfers between devices, body(): lax.psum_scatter(local_grads[1].astype(jnp.bfloat16), 'dp', scatter_dimen...  71.6 us
    all_gather x2, waiting for transfers between devices, body(): lax.all_gather(mix_value.astype(jnp.bfloat16), 'tensor', axis=1, tiled=True)  66.5 us
    all_gather x2, waiting for transfers between devices, fetch_dense(): lax.all_gather(contract_weight[layer_index], 'dp', axis=1, tiled=True)  57.2 us
  transfers between devices with their start and end apart: 31, of which 28 were waited for; matrix products, arithmetic and copies ran while one was open for 11% of the time, Pallas kernels for 0%

commit v1 on v0

--- a/solution.py
+++ b/solution.py
@@ -165,7 +165,17 @@
         dense_pack = fetch_dense(layer_index)
         expand_full, contract_full, ff_gain, ff_shift, con_shift = dense_pack
         ff_value, ff_normed, ff_inverse = layer_norm(middle, ff_gain, ff_shift)
-        ff_rows = lax.all_gather(ff_value.astype(jnp.bfloat16), "tensor", axis=1, tiled=True)
+        x = ff_value.astype(jnp.bfloat16)
+        ways = lax.axis_size("tensor")
+        up = [(d, (d + 1) % ways) for d in range(ways)]
+        down = [(d, (d - 1) % ways) for d in range(ways)]
+        earlier, later = ([x], [x])
+        for _ in range(ways // 2):
+            earlier.append(lax.ppermute(earlier[-1], "tensor", up))
+        for _ in range((ways - 1) // 2):
+            later.append(lax.ppermute(later[-1], "tensor", down))
+        line = jnp.concatenate([*earlier[::-1], *later[1:]], axis=1)
+        ff_rows = jnp.roll(line, (lax.axis_index("tensor") - ways // 2) * x.shape[1], axis=1)
         preact = jnp.einsum(
             "bsd,df->bsf", ff_rows, expand_full, preferred_element_type=jnp.float32
         ) + expbias[layer_index].astype(jnp.float32)

time: 1480 us -> 1400 us (0.946)
  waiting for transfers between devices: 1040 us -> 922 us
  starting transfers between devices: 3.42 us -> 24.1 us
  other arithmetic: 51.7 us -> 66.8 us
    all_gather x2 -> x0, waiting for transfers between devices: 80.1 us -> none  [body(): lax.all_gather(ff_value.astype(jnp.bfloat16), 'tensor', axis=1, tiled=True)]
    all_gather x2, waiting for transfers between devices: 55.3 us -> 0.02 us  [fetch_dense(): lax.all_gather(expand_weight[layer_index], 'dp', axis=0, tiled=True)]
    ppermute x0 -> x6, waiting for transfers between devices: none -> 36.2 us  [the longest x4 33.4 us: body(): earlier.append(lax.ppermute(earlier[-1], 'tensor', up))]
    ppermute x0 -> x6, starting transfers between devices: none -> 21.7 us  [the longest x4 20.7 us: body(): earlier.append(lax.ppermute(earlier[-1], 'tensor', up))]
    another operation x0 -> x2, other arithmetic: none -> 17.5 us
    unnamed x41 -> x39, waiting for transfers between devices: 321 us -> 319 us
    unnamed x182 -> x226, local copies, waits for them, and re-layouts: 42.8 us -> 44.4 us
  transfers between devices with their start and end apart: 31 -> 35, of which waited for: 28 -> 30; matrix products, arithmetic and copies ran while one was open for 11% -> 13% of each run, Pallas kernels for 0% -> 0%
where the time goes in v1:
time: 1400 us
  waiting for transfers between devices  922 us (66%)
  matrix products  216 us (15%)
  blocking collectives  89.4 us (6%)
  other arithmetic  66.8 us (5%)
  local copies, waits for them, and re-layouts  60.9 us (4%)
  starting transfers between devices  24.1 us (2%)
  between operations  16.8 us (1%)
    unnamed x39, waiting for transfers between devices  319 us
    psum x1, waiting for transfers between devices, body(): lax.psum((jnp.stack(vector_list), jnp.stack(expbias_list)), ('dp', 'tenso...  124 us
    reduce_scatter x2, waiting for transfers between devices, body(): lax.psum_scatter(local_grads[2].astype(jnp.bfloat16), 'dp', scatter_dimen...  90.7 us
    reduce_scatter x2, waiting for transfers between devices, body(): lax.psum_scatter(local_grads[1].astype(jnp.bfloat16), 'dp', scatter_dimen...  71.5 us
    all_gather x2, waiting for transfers between devices, body(): lax.all_gather(mix_value.astype(jnp.bfloat16), 'tensor', axis=1, tiled=True)  66.2 us
    all_gather x2, waiting for transfers between devices, body(): upstream_rows = lax.all_gather(upstream_half, 'tensor', axis=1, tiled=True)  62.8 us
    all_gather x2, waiting for transfers between devices, fetch_dense(): lax.all_gather(contract_weight[layer_index], 'dp', axis=1, tiled=True)  50.4 us
    all_gather x2, waiting for transfers between devices, fetch_attention(): lax.all_gather(inproj_weight[layer_index], 'dp', axis=1, tiled=True)  47.9 us
  transfers between devices with their start and end apart: 35, of which 30 were waited for; matrix products, arithmetic and copies ran while one was open for 13% of the time, Pallas kernels for 0%

profile of v1, /device:TPU:8, one launch (start us, length us, event | category | flops | bytes accessed | tf_op | source)
XLA Modules:
  0.0 1396.0 jit_solution(16911296004720124499)
XLA Ops:
  19.3 25.2 %all-reduce.20 = (bf16[1152]{0:T(1024)(128)(2,1)S(1)}, bf16[1152]{0:T(1024)(128)(2,1)S(1)}, bf16[1152]{0:T(1024)(128)(2,1)S(1)}, bf16[1152]{0:T(1024)(128)(2,1)S...) all-reduce(bf16[1152]{0:T(1024)(128)(2,1)S(1)} %dynamic-update-slic, ...), channel_id=3, replica_groups=mesh['dp'=8,'tensor'=4] {'dp'}, use_global_device_ids=true, to_apply=%add.1 | all-reduce | flops 13824 | bytes 55296
  48.7 10.2 all-gather.3
  58.8 25.9 %all-gather.33.cloned.1.call-done = bf16[1,736,1152]{2,1,0:T(8,128)(2,1)} async-done(((bf16[1,184,1152]{2,1,0:T(8,128)(2,1)}), bf16[1,736,1152]{2,1,0:T(8,128)(2,1)}) %all-gather.33.cloned.1.call-update) | async-done | bytes 1695760 | tf_op jit(solution)/shard_map/all_gather | solution.py:138
  84.8 32.5 %all-gather.45.cloned.1.call-done = bf16[1,3,1152,288]{3,2,1,0:T(8,128)(2,1)} async-done(((bf16[1,3,144,288]{3,2,1,0:T(8,128)(2,1)}), bf16[1,3,1152,288]{3,2,1,0:T(8,128)(2,1)}) %all-gather.45.cloned.1.call-update) | async-done | bytes 1990672 | tf_op jit(solution)/shard_map/all_gather | solution.py:116
  117.3 4.2 fusion.92
  137.1 34.5 %reduce-scatter.61.cloned.1.call-done = bf16[1,184,1152]{2,1,0:T(8,128)(2,1)} async-done(((bf16[1,736,1152]{2,1,0:T(8,128)(2,1)}), bf16[1,184,1152]{2,1,0:T(8,128)(2,1)}) %reduce-scatter.61.cloned.1.call-update) | async-done | bytes 423952
  175.3 10.6 collective-permute-done
  186.0 8.9 collective-permute-start.1
  197.3 5.7 collective-permute-done.1
  203.0 7.7 fusion.110
  210.8 6.5 convolution_add_fusion.1
  217.3 18.6 %all-gather.49.cloned.1.call-done = bf16[1,1076,1152]{1,2,0:T(8,128)(2,1)} async-done(((bf16[1,1076,144]{1,2,0:T(8,128)(2,1)}), bf16[1,1076,1152]{1,2,0:T(8,128)(2,1)}) %all-gather.49.cloned.1.call-update) | async-done | bytes 2479120 | tf_op jit(solution)/shard_map/all_gather | solution.py:126
  235.9 7.2 fusion.70
  244.0 35.7 %reduce-scatter.63.cloned.1.call-done = bf16[1,184,1152]{2,1,0:T(8,128)(2,1)} async-done(((bf16[1,736,1152]{2,1,0:T(8,128)(2,1)}), bf16[1,184,1152]{2,1,0:T(8,128)(2,1)}) %reduce-scatter.63.cloned.1.call-update) | async-done | bytes 423952
  282.4 14.0 %all-gather.13 = bf16[1,288,1152]{1,2,0:T(8,128)(2,1)} all-gather(bf16[1,288,144]{1,2,0:T(8,128)(2,1)S(1)} %get-tuple-element.125), channel_id=15, replica_groups=mesh['dp'=8,'tensor'=4] {'dp'}, dimensions={2}, use_global_device_ids=true | all-gather | bytes 746496 | tf_op jit(solution)/shard_map/all_gather | solution.py:117
  296.4 15.4 %all-gather.51.cloned.1.call-done = bf16[1,3,1152,288]{3,2,1,0:T(8,128)(2,1)} async-done(((bf16[1,3,144,288]{3,2,1,0:T(8,128)(2,1)}), bf16[1,3,1152,288]{3,2,1,0:T(8,128)(2,1)}) %all-gather.51.cloned.1.call-update) | async-done | bytes 1990672 | tf_op jit(solution)/shard_map/all_gather | solution.py:116
  311.8 40.2 %all-gather.35.cloned.1.call-done = bf16[1,736,1152]{2,1,0:T(8,128)(2,1)} async-done(((bf16[1,184,1152]{2,1,0:T(8,128)(2,1)}), bf16[1,736,1152]{2,1,0:T(8,128)(2,1)}) %all-gather.35.cloned.1.call-update) | async-done | bytes 1695760 | tf_op jit(solution)/shard_map/all_gather | solution.py:138
  352.0 4.3 fusion.95
  372.1 34.2 %reduce-scatter.65.cloned.1.call-done = bf16[1,184,1152]{2,1,0:T(8,128)(2,1)} async-done(((bf16[1,736,1152]{2,1,0:T(8,128)(2,1)}), bf16[1,184,1152]{2,1,0:T(8,128)(2,1)}) %reduce-scatter.65.cloned.1.call-update) | async-done | bytes 423952
  410.1 10.6 collective-permute-done.3
  420.7 8.7 collective-permute-start.4
  431.2 6.4 collective-permute-done.4
  437.6 9.7 fusion.102
  447.4 6.6 convolution_add_fusion
  454.0 25.0 %all-gather.37.cloned.1.call-done = bf16[1,736,1152]{2,1,0:T(8,128)(2,1)} async-done(((bf16[1,184,1152]{2,1,0:T(8,128)(2,1)}), bf16[1,736,1152]{2,1,0:T(8,128)(2,1)}) %all-gather.37.cloned.1.call-update) | async-done | bytes 1695760 | tf_op jit(solution)/shard_map/all_gather | solution.py:235
  479.0 31.7 %all-gather.55.cloned.1.call-done = bf16[1,1076,1152]{1,2,0:T(8,128)(2,1)} async-done(((bf16[1,1076,144]{1,2,0:T(8,128)(2,1)}), bf16[1,1076,1152]{1,2,0:T(8,128)(2,1)}) %all-gather.55.cloned.1.call-update) | async-done | bytes 2479120 | tf_op jit(solution)/shard_map/all_gather | solution.py:126
  510.7 8.2 fusion.246
  524.3 7.2 fusion.71
  531.6 29.0 %reduce-scatter.69.cloned.1.call-done = bf16[1,184,1152]{2,1,0:T(8,128)(2,1)} async-done(((bf16[1,736,1152]{2,1,0:T(8,128)(2,1)}), bf16[1,184,1152]{2,1,0:T(8,128)(2,1)}) %reduce-scatter.69.cloned.1.call-update) | async-done | bytes 423952
  562.7 36.5 %reduce-scatter.67.cloned.1.call-done = bf16[1,184,1152]{2,1,0:T(8,128)(2,1)} async-done(((bf16[1,736,1152]{2,1,0:T(8,128)(2,1)}), bf16[1,184,1152]{2,1,0:T(8,128)(2,1)}) %reduce-scatter.67.cloned.1.call-update) | async-done | bytes 423952
  604.3 38.2 %all-gather.39.cloned.1.call-done = bf16[1,736,1152]{2,1,0:T(8,128)(2,1)} async-done(((bf16[1,184,1152]{2,1,0:T(8,128)(2,1)}), bf16[1,736,1152]{2,1,0:T(8,128)(2,1)}) %all-gather.39.cloned.1.call-update) | async-done | bytes 1695760 | tf_op jit(solution)/shard_map/all_gather | solution.py:257
  644.9 5.1 fusion.235
  650.0 5.0 fusion.188
  655.0 17.1 %fusion.134 = bf16[4,72,736]{2,1,0:T(8,128)(2,1)S(1)} fusion(f32[4,736,736]{1,2,0:T(8,128)} %fusion.188, f32[4,736,736]{1,2,0:T(8,128)} %copy-done.1, f32[4,736]{1,0:T(4,128)S(1)} %log_add_fusion, pred[736]{0:T(1024)(128)(4,1)S(1)} %compare_reduce_fusion, f32[736,4,72]{0,2,1:T(8,128)} %bitcast.270, f32[4,72]{1,0:T(4,128)S(1)} %copy-done.69), kind=kOutput, calls=%fused_computation.166 | convolution fusion | flops 336491104 | bytes 18619744 | tf_op jit(solution)/shard_map/bhqk,bqhd->bkhd/dot_general | solution.py:75
  672.1 17.6 %fusion.236 = (f32[4,72]{1,0:T(4,128)}, bf16[1,736,4,72]{1,3,2,0:T(8,128)(2,1)S(1)}) fusion(bf16[736,4,72]{0,2,1:T(8,128)(2,1)S(1)} %bitcast.280, f32[4,736,736]{1,2,0:T(8,128)} %fusion.188, f32[4,736,736]{1,2,0:T(8,128)} %copy-done.1, f32[4,736]{1,0:T(4,128)S(1)} %log_add_fusion, pred[736]{0:T(1024)(128)(4,1)S(1)} %compare_reduce_fusion), kind=kOutput, calls=%fused_computation.325 | convolution fusion | flops 336278848 | bytes 18195808 | tf_op jit(solution)/shard_map/bhqk,bkhd->bqhd/dot_general | solution.py:72
  689.8 5.9 fusion.75
  695.7 36.3 %reduce-scatter.71.cloned.1.call-done = bf16[1,184,1152]{2,1,0:T(8,128)(2,1)} async-done(((bf16[1,736,1152]{2,1,0:T(8,128)(2,1)}), bf16[1,184,1152]{2,1,0:T(8,128)(2,1)}) %reduce-scatter.71.cloned.1.call-update) | async-done | bytes 423952
  737.4 37.8 %all-gather.41.cloned.1.call-done = bf16[1,736,1152]{2,1,0:T(8,128)(2,1)} async-done(((bf16[1,184,1152]{2,1,0:T(8,128)(2,1)}), bf16[1,736,1152]{2,1,0:T(8,128)(2,1)}) %all-gather.41.cloned.1.call-update) | async-done | bytes 1695760 | tf_op jit(solution)/shard_map/all_gather | solution.py:235
  775.1 8.2 fusion.247
  784.6 4.0 fusion.73
  788.6 36.3 %reduce-scatter.73.cloned.1.call-done = bf16[1,184,1152]{2,1,0:T(8,128)(2,1)} async-done(((bf16[1,736,1152]{2,1,0:T(8,128)(2,1)}), bf16[1,184,1152]{2,1,0:T(8,128)(2,1)}) %reduce-scatter.73.cloned.1.call-update) | async-done | bytes 423952
  830.8 4.8 fusion.69
  835.7 6.0 copy.81
  841.7 4.2 reshape.929
  846.2 6.8 convolution_convert_fusion
  853.0 6.3 convolution_convert_fusion.1
  859.4 5.7 convolution_convert_fusion.2
  865.2 5.6 convolution_convert_fusion.3
  877.2 5.1 fusion.186
  882.3 16.6 %fusion.137 = bf16[4,72,736]{2,1,0:T(8,128)(2,1)S(1)} fusion(f32[4,736,736]{1,2,0:T(8,128)} %fusion.186, f32[4,736,736]{1,2,0:T(8,128)} %copy-done, f32[4,736]{1,0:T(4,128)S(1)} %copy-done.42, pred[736]{0:T(1024)(128)(4,1)S(1)} %compare_reduce_fusion, f32[736,4,72]{0,2,1:T(8,128)S(1)} %bitcast.268, f32[4,72]{1,0:T(4,128)S(1)} %copy-done.67), kind=kOutput, calls=%fused_computation.167 | convolution fusion | flops 336491104 | bytes 18619744 | tf_op jit(solution)/shard_map/bhqk,bqhd->bkhd/dot_general | solution.py:75
  902.7 17.4 %fusion.234 = (f32[4,72]{1,0:T(4,128)}, bf16[1,736,4,72]{1,3,2,0:T(8,128)(2,1)S(1)}) fusion(bf16[736,4,72]{0,2,1:T(8,128)(2,1)S(1)} %bitcast.278, f32[4,736,736]{1,2,0:T(8,128)} %fusion.186, f32[4,736,736]{1,2,0:T(8,128)} %copy-done, f32[4,736]{1,0:T(4,128)S(1)} %copy-done.42, pred[736]{0:T(1024)(128)(4,1)S(1)} %compare_reduce_fusion), kind=kOutput, calls=%fused_computation.323 | convolution fusion | flops 336278848 | bytes 18195808 | tf_op jit(solution)/shard_map/bhqk,bkhd->bqhd/dot_general | solution.py:72
  920.1 4.8 fusion.233
  928.9 6.0 copy.79
  934.9 4.2 reshape.927
  939.5 6.1 fusion.74
  950.5 39.9 %psum.15 = f32[2,4304]{1,0:T(2,128)S(1)} all-reduce(f32[2,4304]{1,0:T(2,128)S(1)} %pad_maximum_fusion.7), channel_id=1, replica_groups=mesh['dp'=8,'tensor'=4] {'dp','tensor'}, use_global_device_ids=true, to_apply=%region_55.57 | all-reduce | flops 8608 | bytes 68864 | tf_op jit(solution)/shard_map/psum | solution.py:347
  991.2 15.1 %reduce-scatter.53.cloned.1.call-done = bf16[1076,144]{0,1:T(8,128)(2,1)} async-done(((bf16[1076,1152]{0,1:T(8,128)(2,1)}), bf16[1076,144]{0,1:T(8,128)(2,1)}) %reduce-scatter.53.cloned.1.call-update) | async-done | bytes 309904 | tf_op jit(solution)/shard_map/reduce_scatter | solution.py:321
  1008.5 44.3 %reduce-scatter.51.cloned.1.call-done = bf16[144,1076]{1,0:T(8,128)(2,1)} async-done(((bf16[1152,1076]{1,0:T(8,128)(2,1)}), bf16[144,1076]{1,0:T(8,128)(2,1)}) %reduce-scatter.51.cloned.1.call-update) | async-done | bytes 309904 | tf_op jit(solution)/shard_map/reduce_scatter | solution.py:318
  1052.8 46.4 %reduce-scatter.49.cloned.1.call-done = bf16[144,1076]{1,0:T(8,128)(2,1)} async-done(((bf16[1152,1076]{1,0:T(8,128)(2,1)}), bf16[144,1076]{1,0:T(8,128)(2,1)}) %reduce-scatter.49.cloned.1.call-update) | async-done | bytes 309904 | tf_op jit(solution)/shard_map/reduce_scatter | solution.py:318
  1103.8 33.2 %reduce-scatter.47.cloned.1.call-done = bf16[288,144]{0,1:T(8,128)(2,1)} async-done(((bf16[288,1152]{0,1:T(8,128)(2,1)}), bf16[288,144]{0,1:T(8,128)(2,1)}) %reduce-scatter.47.cloned.1.call-update) | async-done | bytes 82960 | tf_op jit(solution)/shard_map/reduce_scatter | solution.py:315
  1137.0 38.3 %reduce-scatter.45.cloned.1.call-done = bf16[288,144]{0,1:T(8,128)(2,1)} async-done(((bf16[288,1152]{0,1:T(8,128)(2,1)}), bf16[288,144]{0,1:T(8,128)(2,1)}) %reduce-scatter.45.cloned.1.call-update) | async-done | bytes 82960 | tf_op jit(solution)/shard_map/reduce_scatter | solution.py:315
  1177.1 41.6 %reduce-scatter.57.cloned.1.call-done = bf16[144,864]{1,0:T(8,128)(2,1)} async-done(((bf16[1152,864]{1,0:T(8,128)(2,1)}), bf16[144,864]{1,0:T(8,128)(2,1)}) %reduce-scatter.57.cloned.1.call-update) | async-done | bytes 248848
  1224.5 32.9 %reduce-scatter.75.cloned.1.call-done = bf16[1,184,1152]{2,1,0:T(8,128)(2,1)} async-done(((bf16[1,736,1152]{2,1,0:T(8,128)(2,1)}), bf16[1,184,1152]{2,1,0:T(8,128)(2,1)}) %reduce-scatter.75.cloned.1.call-update) | async-done | bytes 423952
  1262.7 123.6 %all-reduce.23.cloned.1.call-done = f32[2,8,1152]{2,0,1:T(2,128)} async-done(((f32[2,8,1152]{2,0,1:T(2,128)}), f32[2,8,1152]{2,0,1:T(2,128)}) %all-reduce.23.cloned.1.call-update) | async-done | bytes 73744 | tf_op jit(solution)/shard_map/psum | solution.py:347
  (425 shorter events, 131.9 us)
Async XLA Ops:
  7.2 40.2 %copy-start.30 = (bf16[2,3,144,288]{3,2,1,0:T(8,128)(2,1)S(1)}, bf16[2,3,144,288]{3,2,1,0:T(8,128)(2,1)}, u32[]{:S(2)}) copy-start(bf16[2,3,144,288]{3,2,1,0:T(8,128)(2,1)} %param.22) | copy-start | bytes 1492996
  7.2 41.2 %copy-start.73 = (bf16[2,288]{1,0:T(2,128)(2,1)S(1)}, bf16[2,288]{1,0:T(2,128)(2,1)}, u32[]{:S(2)}) copy-start(bf16[2,288]{1,0:T(2,128)(2,1)} %param.23) | copy-start | bytes 3460
  7.2 41.3 %copy-start.74 = (bf16[2,288]{1,0:T(2,128)(2,1)S(1)}, bf16[2,288]{1,0:T(2,128)(2,1)}, u32[]{:S(2)}) copy-start(bf16[2,288]{1,0:T(2,128)(2,1)} %param.24) | copy-start | bytes 3460
  7.2 41.4 %copy-start.82 = (s32[1,736]{1,0:T(1,128)S(1)}, s32[1,736]{1,0:T(1,128)}, u32[]{:S(2)}) copy-start(s32[1,736]{1,0:T(1,128)} %param.19) | copy-start | bytes 8836
  7.2 41.4 %copy-start.38 = (bf16[2,288,144]{1,2,0:T(8,128)(2,1)S(1)}, bf16[2,288,144]{1,2,0:T(8,128)(2,1)}, u32[]{:S(2)}) copy-start(bf16[2,288,144]{1,2,0:T(8,128)(2,1)} %param.25) | copy-start | bytes 497668
  7.2 77.6 %all-gather.33.cloned.1.call-start = ((), (), s32[]{:S(2)}) async-start(), calls=%async_computation.16 | async-start | bytes 2119680 | tf_op jit(solution)/shard_map/all_gather | solution.py:138
  8.6 39.9 %copy-start.52 = (f32[184]{0:T(256)}, f32[184]{0:T(256)S(1)}, u32[]{:S(2)}) copy-start(f32[184]{0:T(256)S(1)} %broadcast_multiply_fusion.11) | copy-start | bytes 2212
  10.1 38.5 %copy-start.58 = (f32[184]{0:T(256)}, f32[184]{0:T(256)S(1)}, u32[]{:S(2)}) copy-start(f32[184]{0:T(256)S(1)} %add_rsqrt_fusion.3) | copy-start | bytes 2212
  47.3 69.9 %all-gather.45.cloned.1.call-start = ((), (), s32[]{:S(2)}) async-start(), calls=%async_computation.29 | async-start | bytes 2985984 | tf_op jit(solution)/shard_map/all_gather | solution.py:116
  48.3 123.2 %reduce-scatter.61.cloned.1.call-start = ((), (), s32[]{:S(2)}) async-start(), calls=%async_computation.37 | async-start | bytes 2119680
  48.5 73.2 %copy-start.66 = (f32[4,72]{1,0:T(4,128)}, f32[4,72]{1,0:T(4,128)S(1)}, u32[]{:S(2)}) copy-start(f32[4,72]{1,0:T(4,128)S(1)} %reshape.786) | copy-start | bytes 3460
  58.8 73.0 %copy-start.27 = (bf16[1,288,1152]{1,2,0:T(8,128)(2,1)}, bf16[1,288,1152]{1,2,0:T(8,128)(2,1)S(1)}, u32[]{:S(2)}) copy-start(bf16[1,288,1152]{1,2,0:T(8,128)(2,1)S(1)} %all-gather.3) | copy-start | bytes 1990660
  135.0 75.7 %all-gather.47.cloned.1.call-start = ((), (), s32[]{:S(2)}) async-start(), calls=%async_computation.30 | async-start | bytes 2985984 | tf_op jit(solution)/shard_map/all_gather | solution.py:125
  136.0 58.8 %copy-start.57 = (bf16[2,1076]{1,0:T(2,128)(2,1)S(1)}, bf16[2,1076]{1,0:T(2,128)(2,1)}, u32[]{:S(2)}) copy-start(bf16[2,1076]{1,0:T(2,128)(2,1)} %param.30) | copy-start | bytes 12916
  136.0 99.9 %all-gather.49.cloned.1.call-start = ((), (), s32[]{:S(2)}) async-start(), calls=%async_computation.31 | async-start | bytes 2985984 | tf_op jit(solution)/shard_map/all_gather | solution.py:126
  137.0 142.7 %reduce-scatter.63.cloned.1.call-start = ((), (), s32[]{:S(2)}) async-start(), calls=%async_computation.38 | async-start | bytes 2119680
  173.0 44.3 %copy-start.60 = (f32[184]{0:T(256)}, f32[184]{0:T(256)S(1)}, u32[]{:S(2)}) copy-start(f32[184]{0:T(256)S(1)} %add_rsqrt_fusion.2) | copy-start | bytes 2212
  173.3 12.7 collective-permute-start
  174.8 21.7 %collective-permute-start.2 = (bf16[1,184,1152]{2,1,0:T(8,128)(2,1)S(1)}, bf16[1,184,1152]{2,1,0:T(8,128)(2,1)S(1)}, u32[]{:S(2)}, u32[]{:S(2)}) collective-permute-start(bf16[1,184,1152]{2,1,0:T(8,128)(2,1)S(1)} %add_convert_fusion.6), channel_id=1, source_target_pairs={{0,3},{1,0},{2,1},{3,2},{4,7},{5,4},{6,5},{7,6},{8,11},{9,8},{10,9... | collective-permute-start | bytes 1271816 | tf_op jit(solution)/shard_map/ppermute | solution.py:176
  186.0 17.0 %collective-permute-start.1 = (bf16[1,184,1152]{2,1,0:T(8,128)(2,1)S(1)}, bf16[1,184,1152]{2,1,0:T(8,128)(2,1)}, u32[]{:S(2)}, u32[]{:S(2)}) collective-permute-start(bf16[1,184,1152]{2,1,0:T(8,128)(2,1)S(1)} %collective-permute-done), channel_id=1, source_target_pairs={{0,1},{1,2},{2,3},{3,0},{4,5},{5,6},{6,7},{7,4},{8,9},{9,10},{10,1... | collective-permute-start | bytes 1271816 | tf_op jit(solution)/shard_map/ppermute | solution.py:174
  243.1 68.7 %all-gather.51.cloned.1.call-start = ((), (), s32[]{:S(2)}) async-start(), calls=%async_computation.32 | async-start | bytes 2985984 | tf_op jit(solution)/shard_map/all_gather | solution.py:116
  243.9 108.2 %all-gather.35.cloned.1.call-start = ((), (), s32[]{:S(2)}) async-start(), calls=%async_computation.17 | async-start | bytes 2119680 | tf_op jit(solution)/shard_map/all_gather | solution.py:138
  280.9 75.4 %copy-start.54 = (f32[184]{0:T(256)}, f32[184]{0:T(256)S(1)}, u32[]{:S(2)}) copy-start(f32[184]{0:T(256)S(1)} %broadcast_multiply_fusion.9) | copy-start | bytes 2212
  281.1 75.2 %copy-start.62 = (f32[184]{0:T(256)}, f32[184]{0:T(256)S(1)}, u32[]{:S(2)}) copy-start(f32[184]{0:T(256)S(1)} %add_rsqrt_fusion.1) | copy-start | bytes 2212
  282.1 124.2 %reduce-scatter.65.cloned.1.call-start = ((), (), s32[]{:S(2)}) async-start(), calls=%async_computation.39 | async-start | bytes 2119680
  282.3 74.2 %copy-start.68 = (f32[4,72]{1,0:T(4,128)}, f32[4,72]{1,0:T(4,128)S(1)}, u32[]{:S(2)}) copy-start(f32[4,72]{1,0:T(4,128)S(1)} %reshape.789) | copy-start | bytes 3460
  369.9 77.5 %all-gather.53.cloned.1.call-start = ((), (), s32[]{:S(2)}) async-start(), calls=%async_computation.33 | async-start | bytes 2985984 | tf_op jit(solution)/shard_map/all_gather | solution.py:125
  370.5 108.5 %all-gather.37.cloned.1.call-start = ((), (), s32[]{:S(2)}) async-start(), calls=%async_computation.18 | async-start | bytes 2119680 | tf_op jit(solution)/shard_map/all_gather | solution.py:235
  371.4 139.3 %all-gather.55.cloned.1.call-start = ((), (), s32[]{:S(2)}) async-start(), calls=%async_computation.34 | async-start | bytes 2985984 | tf_op jit(solution)/shard_map/all_gather | solution.py:126
  372.0 188.6 %reduce-scatter.69.cloned.1.call-start = ((), (), s32[]{:S(2)}) async-start(), calls=%async_computation.41 | async-start | bytes 2119680
  372.1 75.3 %copy-start.70 = (f32[1076]{0:T(1024)S(1)}, f32[1076]{0:T(1024)}, u32[]{:S(2)}) copy-start(f32[1076]{0:T(1024)} %get-tuple-element.62) | copy-start | bytes 12916
  408.0 12.7 collective-permute-start.3
  409.6 21.7 %collective-permute-start.5 = (bf16[1,184,1152]{2,1,0:T(8,128)(2,1)S(1)}, bf16[1,184,1152]{2,1,0:T(8,128)(2,1)S(1)}, u32[]{:S(2)}, u32[]{:S(2)}) collective-permute-start(bf16[1,184,1152]{2,1,0:T(8,128)(2,1)S(1)} %add_convert_fusion.4), channel_id=1, source_target_pairs={{0,3},{1,0},{2,1},{3,2},{4,7},{5,4},{6,5},{7,6},{8,11},{9,8},{10,9... | collective-permute-start | bytes 1271816 | tf_op jit(solution)/shard_map/ppermute | solution.py:176
  420.7 16.9 %collective-permute-start.4 = (bf16[1,184,1152]{2,1,0:T(8,128)(2,1)S(1)}, bf16[1,184,1152]{2,1,0:T(8,128)(2,1)S(1)}, u32[]{:S(2)}, u32[]{:S(2)}) collective-permute-start(bf16[1,184,1152]{2,1,0:T(8,128)(2,1)S(1)} %collective-permute-done.3), channel_id=1, source_target_pairs={{0,1},{1,2},{2,3},{3,0},{4,5},{5,6},{6,7},{7,4},{8,9},{9,10},{10,1... | collective-permute-start | bytes 1271816 | tf_op jit(solution)/shard_map/ppermute | solution.py:174
  524.1 75.1 %reduce-scatter.67.cloned.1.call-start = ((), (), s32[]{:S(2)}) async-start(), calls=%async_computation.40 | async-start | bytes 2119680
  531.6 110.9 %all-gather.39.cloned.1.call-start = ((), (), s32[]{:S(2)}) async-start(), calls=%async_computation.19 | async-start | bytes 2119680 | tf_op jit(solution)/shard_map/all_gather | solution.py:257
  604.2 127.8 %reduce-scatter.71.cloned.1.call-start = ((), (), s32[]{:S(2)}) async-start(), calls=%async_computation.42 | async-start | bytes 2119680
  689.8 42.3 %copy-start.55 = (f32[184]{0:T(256)S(1)}, f32[184]{0:T(256)}, u32[]{:S(2)}) copy-start(f32[184]{0:T(256)} %copy-done.54) | copy-start | bytes 2212
  689.8 42.3 %copy-start.63 = (f32[184]{0:T(256)S(1)}, f32[184]{0:T(256)}, u32[]{:S(2)}) copy-start(f32[184]{0:T(256)} %copy-done.62) | copy-start | bytes 2212
  695.6 38.5 %copy-start.11 = (f32[1,184,1152]{2,1,0:T(8,128)S(1)}, f32[1,184,1152]{2,1,0:T(8,128)}, u32[]{:S(2)}) copy-start(f32[1,184,1152]{2,1,0:T(8,128)} %copy-done.10) | copy-start | bytes 2543620
  695.7 79.5 %all-gather.41.cloned.1.call-start = ((), (), s32[]{:S(2)}) async-start(), calls=%async_computation.20 | async-start | bytes 2119680 | tf_op jit(solution)/shard_map/all_gather | solution.py:235
  736.9 88.0 %reduce-scatter.73.cloned.1.call-start = ((), (), s32[]{:S(2)}) async-start(), calls=%async_computation.43 | async-start | bytes 2119680
  784.6 40.4 %copy-start.61 = (f32[184]{0:T(256)S(1)}, f32[184]{0:T(256)}, u32[]{:S(2)}) copy-start(f32[184]{0:T(256)} %copy-done.60) | copy-start | bytes 2212
  788.6 42.3 %copy-start.34 = (bf16[1,736,4,72]{1,3,2,0:T(8,128)(2,1)S(1)}, bf16[1,736,4,72]{1,3,2,0:T(8,128)(2,1)}, u32[]{:S(2)}) copy-start(bf16[1,736,4,72]{1,3,2,0:T(8,128)(2,1)} %get-tuple-element.113) | copy-start | bytes 1271812
  788.6 42.3 %copy-start.90 = (bf16[4,72,736]{2,1,0:T(8,128)(2,1)S(1)}, bf16[4,72,736]{2,1,0:T(8,128)(2,1)}, u32[]{:S(2)}) copy-start(bf16[4,72,736]{2,1,0:T(8,128)(2,1)} %copy-done.89) | copy-start | bytes 1271812
  788.6 86.3 %all-gather.43.cloned.1.call-start = ((), (), s32[]{:S(2)}) async-start(), calls=%async_computation.21 | async-start | bytes 2119680 | tf_op jit(solution)/shard_map/all_gather | solution.py:257
  830.8 116.3 %reduce-scatter.59.cloned.1.call-start = ((), (), s32[]{:S(2)}) async-start(), calls=%async_computation.36 | async-start | bytes 2322432
  846.0 145.2 %reduce-scatter.55.cloned.1.call-start = ((), (), s32[]{:S(2)}) async-start(), calls=%async_computation.28 | async-start | bytes 2985984 | tf_op jit(solution)/shard_map/reduce_scatter | solution.py:321
  853.0 153.3 %reduce-scatter.53.cloned.1.call-start = ((), (), s32[]{:S(2)}) async-start(), calls=%async_computation.27 | async-start | bytes 2985984 | tf_op jit(solution)/shard_map/reduce_scatter | solution.py:321
  859.4 193.4 %reduce-scatter.51.cloned.1.call-start = ((), (), s32[]{:S(2)}) async-start(), calls=%async_computation.26 | async-start | bytes 2985984 | tf_op jit(solution)/shard_map/reduce_scatter | solution.py:318
  865.1 234.0 %reduce-scatter.49.cloned.1.call-start = ((), (), s32[]{:S(2)}) async-start(), calls=%async_computation.25 | async-start | bytes 2985984 | tf_op jit(solution)/shard_map/reduce_scatter | solution.py:318
  870.8 266.2 %reduce-scatter.47.cloned.1.call-start = ((), (), s32[]{:S(2)}) async-start(), calls=%async_computation.24 | async-start | bytes 995328 | tf_op jit(solution)/shard_map/reduce_scatter | solution.py:315
  874.6 300.7 %reduce-scatter.45.cloned.1.call-start = ((), (), s32[]{:S(2)}) async-start(), calls=%async_computation.23 | async-start | bytes 995328 | tf_op jit(solution)/shard_map/reduce_scatter | solution.py:315
  902.6 316.0 %reduce-scatter.57.cloned.1.call-start = ((), (), s32[]{:S(2)}) async-start(), calls=%async_computation.35 | async-start | bytes 2322432
  939.2 318.2 %reduce-scatter.75.cloned.1.call-start = ((), (), s32[]{:S(2)}) async-start(), calls=%async_computation.44 | async-start | bytes 2119680
  945.5 45.6 %copy-start.50 = (f32[1152]{0:T(1024)S(1)}, f32[1152]{0:T(1024)}, u32[]{:S(2)}) copy-start(f32[1152]{0:T(1024)} %get-tuple-element.46) | copy-start | bytes 13828
  945.6 45.6 %copy-start.51 = (f32[1152]{0:T(1024)S(1)}, f32[1152]{0:T(1024)}, u32[]{:S(2)}) copy-start(f32[1152]{0:T(1024)} %get-tuple-element.94) | copy-start | bytes 13828
  945.6 45.6 %copy-start.49 = (f32[1152]{0:T(1024)S(1)}, f32[1152]{0:T(1024)}, u32[]{:S(2)}) copy-start(f32[1152]{0:T(1024)} %get-tuple-element.58) | copy-start | bytes 13828
  945.6 155.8 %copy-start.65 = (f32[4,72]{1,0:T(4,128)S(1)}, f32[4,72]{1,0:T(4,128)}, u32[]{:S(2)}) copy-start(f32[4,72]{1,0:T(4,128)} %get-tuple-element.108) | copy-start | bytes 3460
  945.6 155.9 %copy-start.84 = (f32[4,72]{1,0:T(4,128)S(1)}, f32[4,72]{1,0:T(4,128)}, u32[]{:S(2)}) copy-start(f32[4,72]{1,0:T(4,128)} %get-tuple-element.110) | copy-start | bytes 3460
  945.6 440.7 %all-reduce.23.cloned.1.call-start = ((), (), s32[]{:S(2)}) async-start(), calls=%async_computation.22 | async-start | bytes 147456 | tf_op jit(solution)/shard_map/psum | solution.py:347
  1103.8 116.4 %copy-start.56 = (f32[1,1152]{1,0:T(1,128)}, f32[1,1152]{1,0:T(1,128)S(1)}, u32[]{:S(2)}) copy-start(f32[1,1152]{1,0:T(1,128)S(1)} %dynamic_update_slice.24) | copy-start | bytes 13828
  1220.2 37.2 %copy-start.5 = (f32[1,184,1152]{2,1,0:T(8,128)S(1)}, f32[1,184,1152]{2,1,0:T(8,128)}, u32[]{:S(2)}) copy-start(f32[1,184,1152]{2,1,0:T(8,128)} %param.18) | copy-start | bytes 2543620
  1221.4 39.1 %copy-start.9 = (f32[1,184,1152]{2,1,0:T(8,128)S(1)}, f32[1,184,1152]{2,1,0:T(8,128)}, u32[]{:S(2)}) copy-start(f32[1,184,1152]{2,1,0:T(8,128)} %copy-done.8) | copy-start | bytes 2543620
  (67 other events, 568.5 us)
Sparse Core Ops, SparseCore 0:
  47.4 37.3 all-gather.32
  87.3 29.9 all-gather.44
  135.1 36.3 reduce-scatter.60
  173.9 30.1 all-gather.46
  205.8 30.1 all-gather.48
  243.2 36.3 reduce-scatter.62
  281.5 30.2 all-gather.50
  314.0 38.0 all-gather.34
  370.0 36.2 reduce-scatter.64
  408.6 30.1 all-gather.52
  440.9 38.0 all-gather.36
  480.7 29.9 all-gather.54
  524.2 36.3 reduce-scatter.68
  562.8 36.3 reduce-scatter.66
  604.4 38.0 all-gather.38
  695.8 36.2 reduce-scatter.70
  737.1 38.0 all-gather.40
  788.7 36.2 reduce-scatter.72
  830.9 38.0 all-gather.42
  872.2 39.9 reduce-scatter.58
  915.7 43.3 reduce-scatter.54
  962.6 43.6 reduce-scatter.52
  1009.8 42.9 reduce-scatter.50
  1056.1 42.9 reduce-scatter.48
  1102.4 34.5 reduce-scatter.46
  1140.7 34.5 reduce-scatter.44
  1178.5 40.0 reduce-scatter.56
  1221.0 36.3 reduce-scatter.74
  1263.0 123.3 all-reduce.22
